TPU v7x, 256 devices: a whole 4x4x8 slice. The times are simulated.
256 devices in a mesh: subj: 8 (over z_hi, core), slab: 32 (over y, z_lo, x).
Axes of the slice: x: 4, y: 4, z: 8 (z_hi: 4, z_lo: 2; z = z_hi * 2 + z_lo), core: 2. Of those that a mesh axis runs over, the one named last changes fastest.
Arguments:
- template: float32 [128, 128, 512], P('slab', 'subj'), may hold values from -6 to 6
- subject: float32 [8, 128, 128, 512], P('subj', 'slab'), may hold values from -6 to 6
- velocity: float32 [8, 2, 3, 128, 128, 512], P('subj', None, None, 'slab'), may hold values from -0.6 to 0.6
Outputs:
- velocity_grad: float32 [8, 2, 3, 128, 128, 512], P('subj', None, None, 'slab')
- template_grad: float32 [128, 128, 512], P('slab', 'subj')
All inputs are finite; a program needn't handle non-finite values.
Results may differ from a plain program's by a relative error of at most 0.0003.
Values sent between devices are 32-bit elements; how exact they have to be, the bound alone decides.
A program may use at most 128 MiB of HBM per device.

v0:
```python
import jax
import jax.numpy as jnp
from jax import lax
from jax.sharding import PartitionSpec as P

SW = 3


smooth_weight = 1.0
match_weight = 5.0


def extended_2(x, sides, width):
    for axis, dim in sides:
        size, length = (lax.axis_size(axis), x.shape[dim])
        up = [(i, (i + 1) % size) for i in range(size - 1)]
        down = [(j, i) for i, j in up]
        last = lax.slice_in_dim(x, length - width, length, axis=dim)
        initial = lax.slice_in_dim(x, 0, width, axis=dim)
        before = lax.ppermute(last, axis, up)
        after = lax.ppermute(initial, axis, down)
        x = jnp.concatenate([before, x, after], axis=dim)
    return x


def shifted(field, dimension, offset):
    widths = [(0, 0)] * field.ndim
    widths[dimension] = (1, 1)
    padded = jnp.pad(field, widths)
    length = field.shape[dimension]
    return lax.slice_in_dim(padded, 1 + offset, 1 + offset + length, axis=dimension)


def plane_neighbours(field):
    total = jnp.zeros_like(field)
    for dimension in range(field.ndim - 2, field.ndim):
        total = total + shifted(field, dimension, 1) + shifted(field, dimension, -1)
    return total


def body(template, subject, velocity):
    whole = lax.all_gather(template, "subj", axis=1, tiled=True)
    flow_field = velocity[0]
    subject_image = subject[0]
    steps_count = flow_field.shape[0]
    step_size = 1.0 / steps_count
    image = whole
    saved = []
    for step_index in range(steps_count):
        flow_step = flow_field[step_index]
        extended = extended_2(image, (("slab", 0),), 1)
        back_diffs = [
            image - extended[:-2],
            image - shifted(image, 1, -1),
            image - shifted(image, 2, -1),
        ]
        fore_diffs = [
            extended[2:] - image,
            shifted(image, 1, 1) - image,
            shifted(image, 2, 1) - image,
        ]
        saved.append((back_diffs, fore_diffs))
        flux = jnp.zeros_like(image)
        for dimension in range(3):
            flux = (
                flux
                + jnp.maximum(flow_step[dimension], 0.0) * back_diffs[dimension]
                + jnp.minimum(flow_step[dimension], 0.0) * fore_diffs[dimension]
            )
        image = image - step_size * flux
    adjoint = image - subject_image
    sources = [None] * steps_count
    for step_index in reversed(range(steps_count)):
        flow_step = flow_field[step_index]
        back_diffs, fore_diffs = saved[step_index]
        sources[step_index] = jnp.stack(
            [
                -match_weight
                * step_size
                * adjoint
                * jnp.where(
                    flow_step[dimension] >= 0.0, back_diffs[dimension], fore_diffs[dimension]
                )
                for dimension in range(3)
            ]
        )
        positives = [jnp.maximum(flow_step[dimension], 0.0) * adjoint for dimension in range(3)]
        negatives = [jnp.minimum(flow_step[dimension], 0.0) * adjoint for dimension in range(3)]
        borders = extended_2(jnp.stack([positives[0], negatives[0]]), (("slab", 1),), 1)
        total = positives[0] - borders[0, 2:] + (borders[1, :-2] - negatives[0])
        for dimension in range(1, 3):
            total = (
                total
                + (positives[dimension] - shifted(positives[dimension], dimension, 1))
                + (shifted(negatives[dimension], dimension, -1) - negatives[dimension])
            )
        adjoint = adjoint - step_size * total
    source = jnp.stack(sources)
    scale = 1.0 + 6.0 * smooth_weight
    smoothed = source / scale
    for sweep_index in range(SW - 1):
        margin = extended_2(smoothed, (("slab", 2),), 1)
        beside_all = margin[:, :, 2:] + margin[:, :, :-2] + plane_neighbours(smoothed)
        smoothed = (source + smooth_weight * beside_all) / scale
    gradient = flow_field + smoothed
    summed = lax.psum(adjoint, "subj")
    share_rows = summed.shape[1] // lax.axis_size("subj")
    template_part = lax.dynamic_slice_in_dim(
        summed, lax.axis_index("subj") * share_rows, share_rows, 1
    )
    return (gradient[None], template_part)


def solution(mesh):
    return jax.shard_map(
        body,
        mesh=mesh,
        in_specs=(
            P("slab", "subj", None),
            P("subj", "slab", None, None),
            P("subj", None, None, "slab", None, None),
        ),
        out_specs=(P("subj", None, None, "slab", None, None), P("slab", "subj", None)),
        check_vma=False,
    )
```

profile of v0, /device:TPU:24, one launch (start us, length us, event | category | flops | bytes accessed | tf_op | source)
XLA Modules:
  0.0 296.2 jit_solution(5131221404651713987)
XLA Ops:
  7.2 0.0 copy-start.16
  7.2 0.0 all-gather.2.cloned.1.call-start
  7.2 0.7 all-gather.2.cloned.1.call-update
  7.9 0.0 all-reduce.18.cloned.1.call-start
  8.0 33.9 %all-gather.2.cloned.1.call-done = f32[4,128,512]{2,1,0:T(8,128)} async-done(((f32[4,16,512]{2,1,0:T(8,128)}), f32[4,128,512]{2,1,0:T(8,128)}) %all-gather.2.cloned.1.call-update) | async-done | bytes 1048592 | tf_op jit(solution)/shard_map/all_gather | solution.py:42
  41.9 1.2 fusion.81
  43.1 5.9 %collective-permute-start.1 = (f32[1,128,512]{2,1,0:T(8,128)S(1)}, f32[1,128,512]{2,1,0:T(8,128)S(1)}, u32[]{:S(2)}, u32[]{:S(2)}) collective-permute-start(f32[1,128,512]{2,1,0:T(8,128)S(1)} %get-tuple-element.35), channel_id=1, source_target_pairs={{1,0},{2,1},{3,2},{4,3},{5,4},{6,5},{7,6},{8,7},{9,8},{10,9},{11,1... | collective-permute-start | bytes 786440 | tf_op jit(solution)/shard_map/ppermute | solution.py:21
  49.0 1.9 collective-permute-start
  50.9 4.0 %collective-permute-done.1 = f32[1,128,512]{2,1,0:T(8,128)S(1)} collective-permute-done((f32[1,128,512]{2,1,0:T(8,128)S(1)}, f32[1,128,512]{2,1,0:T(8,128)S(1)}, u32[]{:S(2)}, u32[]{:S(2)}) %collective-permute-start.1) | collective-permute-done | bytes 262176 | tf_op jit(solution)/shard_map/ppermute | solution.py:21
  55.0 7.1 %collective-permute-done = f32[1,128,512]{2,1,0:T(8,128)S(1)} collective-permute-done((f32[1,128,512]{2,1,0:T(8,128)S(1)}, f32[1,128,512]{2,1,0:T(8,128)S(1)}, u32[]{:S(2)}, u32[]{:S(2)}) %collective-permute-start) | collective-permute-done | bytes 262176 | tf_op jit(solution)/shard_map/ppermute | solution.py:20
  62.1 5.8 %fusion.68 = f32[4,128,512]{2,1,0:T(8,128)S(1)} fusion(f32[4,128,512]{2,1,0:T(8,128)} %all-gather.2.cloned.1.call-done, f32[1,2,3,4,128,512]{5,4,3,2,1,0:T(8,128)} %param.5, f32[1,128,512]{2,1,0:T(8,128)S(1)} %collective-permute-done, f32[1,128,512]{2,1,0:T(8,128)S(1)} %collective-permute-done.1), kind=kLoop, calls=%fused_computation.126 | loop fusion | flops 7077888 | bytes 5767168 | tf_op jit(solution)/shard_map/sub | solution.py:70
  67.9 1.9 collective-permute-start.2
  69.9 6.9 %collective-permute-start.3 = (f32[1,128,512]{2,1,0:T(8,128)S(1)}, f32[1,128,512]{2,1,0:T(8,128)S(1)}, u32[]{:S(2)}, u32[]{:S(2)}) collective-permute-start(f32[1,128,512]{2,1,0:T(8,128)S(1)} %get-tuple-element.34), channel_id=1, source_target_pairs={{1,0},{2,1},{3,2},{4,3},{5,4},{6,5},{7,6},{8,7},{9,8},{10,9},{11,1... | collective-permute-start | bytes 786440 | tf_op jit(solution)/shard_map/ppermute | solution.py:21
  76.8 3.3 %collective-permute-done.2 = f32[1,128,512]{2,1,0:T(8,128)S(1)} collective-permute-done((f32[1,128,512]{2,1,0:T(8,128)S(1)}, f32[1,128,512]{2,1,0:T(8,128)S(1)}, u32[]{:S(2)}, u32[]{:S(2)}) %collective-permute-start.2) | collective-permute-done | bytes 262176 | tf_op jit(solution)/shard_map/ppermute | solution.py:20
  80.2 0.0 copy-done.15
  80.2 1.2 collective-permute-done.3
  81.3 0.0 copy-done.16
  81.3 0.0 copy-done
  81.3 1.6 fusion.75
  83.0 1.6 multiply_bitcast_fusion.2
  84.6 0.1 pad_maximum_fusion.20
  84.7 7.4 %collective-permute-start.4 = (f32[2,1,128,512]{3,2,1,0:T(8,128)S(1)}, f32[2,1,128,512]{3,2,1,0:T(8,128)S(1)}, u32[]{:S(2)}, u32[]{:S(2)}) collective-permute-start(f32[2,1,128,512]{3,2,1,0:T(8,128)S(1)} %get-tuple-element.31), channel_id=1, source_target_pairs={{1,0},{2,1},{3,2},{4,3},{5,4},{6,5},{7,6},{8,7},{9,8},{10,9},{11,1... | collective-permute-start | bytes 1572872 | tf_op jit(solution)/shard_map/ppermute | solution.py:21
  92.1 1.9 collective-permute-start.5
  94.0 0.4 maximum_bitcast_fusion.1
  94.4 6.9 %collective-permute-done.4 = f32[2,1,128,512]{3,2,1,0:T(8,128)S(1)} collective-permute-done((f32[2,1,128,512]{3,2,1,0:T(8,128)S(1)}, f32[2,1,128,512]{3,2,1,0:T(8,128)S(1)}, u32[]{:S(2)}, u32[]{:S(2)}) %collective-permute-start.4) | collective-permute-done | bytes 524320 | tf_op jit(solution)/shard_map/ppermute | solution.py:21
  101.3 7.1 %collective-permute-done.5 = f32[2,1,128,512]{3,2,1,0:T(8,128)S(1)} collective-permute-done((f32[2,1,128,512]{3,2,1,0:T(8,128)S(1)}, f32[2,1,128,512]{3,2,1,0:T(8,128)S(1)}, u32[]{:S(2)}, u32[]{:S(2)}) %collective-permute-start.5) | collective-permute-done | bytes 524320 | tf_op jit(solution)/shard_map/ppermute | solution.py:20
  108.4 0.0 copy-done.17
  108.4 0.8 copy-done.18
  109.2 3.6 %fusion.73 = (f32[1,4,128,512]{3,2,1,0:T(8,128)}, f32[4,128,512]{2,1,0:T(8,128)S(1)}) fusion(f32[1,2,3,4,128,512]{5,4,3,2,1,0:T(8,128)S(1)} %copy-done, f32[4,128,512]{2,1,0:T(8,128)S(1)} %get-tuple-element.5, f32[4,128,512]{2,1,0:T(8,128)S(1)} %get-tuple-element.24, f32[4,128,512]{2,1,0:T(8,128)S(1)} %get-tuple-element.23, ...), kind=kLoop, calls=%fused_computation.147 | loop fusion | flops 6029312 | bytes 12582912 | tf_op jit(solution)/shard_map/stack | solution.py:89
  112.8 0.0 copy-done.10
  112.8 3.9 %fusion.74 = (f32[1,4,128,512]{3,2,1,0:T(8,128)S(1)}, f32[4,128,512]{2,1,0:T(8,128)}, f32[4,128,512]{2,1,0:T(8,128)}, f32[4,128,512]{2,1,0:T(8,128)}, f32[4,128,...) fusion(f32[4,128,512]{2,1,0:T(8,128)S(1)} %get-tuple-element.3,, ...), kind=kLoop, calls=%fused_computation.148 | loop fusion | flops 7340032 | bytes 14155776 | tf_op jit(solution)/shard_map/stack | solution.py:89
  116.8 0.3 maximum_bitcast_fusion
  117.1 0.9 fusion.16
  118.0 0.0 copy-start.3
  118.1 0.3 fusion.79
  118.4 2.1 collective-permute-start.6
  120.4 3.9 %collective-permute-start.7 = (f32[2,3,1,128,512]{4,3,2,1,0:T(8,128)S(1)}, f32[2,3,1,128,512]{4,3,2,1,0:T(8,128)}, u32[]{:S(2)}, u32[]{:S(2)}) collective-permute-start(f32[2,3,1,128,512]{4,3,2,1,0:T(8,128)S(1)} %get-tuple-element.28), channel_id=1, source_target_pairs={{0,1},{1,2},{2,3},{3,4},{4,5},{5,6},{6,7},{7,8},{8,9},{9,10},{10,1... | collective-permute-start | bytes 4718600 | tf_op jit(solution)/shard_map/ppermute | solution.py:20
  124.4 1.1 pad_maximum_fusion.18
  125.5 4.9 %collective-permute-start.10 = (f32[2,1,128,512]{3,2,1,0:T(8,128)}, f32[2,1,128,512]{3,2,1,0:T(8,128)}, u32[]{:S(2)}, u32[]{:S(2)}) collective-permute-start(f32[2,1,128,512]{3,2,1,0:T(8,128)} %get-tuple-element.29), channel_id=1, source_target_pairs={{1,0},{2,1},{3,2},{4,3},{5,4},{6,5},{7,6},{8,7},{9,8},{10,9},{11,1... | collective-permute-start | bytes 1572872 | tf_op jit(solution)/shard_map/ppermute | solution.py:21
  130.4 1.9 collective-permute-start.11
  132.3 25.4 %collective-permute-done.6 = f32[2,3,1,128,512]{4,3,2,1,0:T(8,128)S(1)} collective-permute-done((f32[2,3,1,128,512]{4,3,2,1,0:T(8,128)S(1)}, f32[2,3,1,128,512]{4,3,2,1,0:T(8,128)S(1)}, u32[]{:S(2)}, u32[]{:S(2)}) %collective-permute-start.6) | collective-permute-done | bytes 1572896 | tf_op jit(solution)/shard_map/ppermute | solution.py:21
  157.8 1.2 copy-done.14
  158.9 3.9 %collective-permute-done.7 = f32[2,3,1,128,512]{4,3,2,1,0:T(8,128)} collective-permute-done((f32[2,3,1,128,512]{4,3,2,1,0:T(8,128)S(1)}, f32[2,3,1,128,512]{4,3,2,1,0:T(8,128)}, u32[]{:S(2)}, u32[]{:S(2)}) %collective-permute-start.7) | collective-permute-done | bytes 1572896 | tf_op jit(solution)/shard_map/ppermute | solution.py:20
  162.8 14.6 %fusion.5 = f32[2,3,4,128,512]{4,3,2,1,0:T(8,128)S(1)} fusion(f32[2,3,4,128,512]{4,3,2,1,0:T(8,128)} %copy-done.3, f32[2,3,1,128,512]{4,3,2,1,0:T(8,128)} %collective-permute-done.7, f32[2,3,1,128,512]{4,3,2,1,0:T(8,128)} %copy-done.14, f32[1,3,4,128,512]{4,3,2,1,0:T(8,128)S(1)} %maximum_bitcast_fusion.1, f32[1,3,4,128,512]{4,3,2,1,0:T(8,128)S(1)} %maximum_bitcast_fusion), kind=kLoop, calls=%fused_computation.13 | loop fusion | flops 15728640 | bytes 22020096 | tf_op jit(solution)/shard_map/div | solution.py:104
  177.4 0.0 copy-start.2
  177.5 2.7 copy-done.2
  180.2 2.0 fusion.78
  182.1 2.2 collective-permute-start.8
  184.3 4.1 %collective-permute-start.9 = (f32[2,3,1,128,512]{4,3,2,1,0:T(8,128)}, f32[2,3,1,128,512]{4,3,2,1,0:T(8,128)}, u32[]{:S(2)}, u32[]{:S(2)}) collective-permute-start(f32[2,3,1,128,512]{4,3,2,1,0:T(8,128)} %get-tuple-element.26), channel_id=1, source_target_pairs={{0,1},{1,2},{2,3},{3,4},{4,5},{5,6},{6,7},{7,8},{8,9},{9,10},{10,1... | collective-permute-start | bytes 4718600 | tf_op jit(solution)/shard_map/ppermute | solution.py:20
  188.4 0.0 collective-permute-done.10
  188.4 0.0 collective-permute-done.11
  188.4 0.0 copy-done.5
  188.5 0.0 copy-done.7
  188.5 0.0 copy-done.9
  188.5 0.0 copy-done.11
  188.5 0.0 copy-done.12
  188.5 0.0 copy-done.13
  188.5 4.2 %fusion.35 = f32[4,128,512]{2,1,0:T(8,128)} fusion(f32[4,128,512]{2,1,0:T(8,128)S(1)} %copy-done.7, f32[4,128,512]{2,1,0:T(8,128)} %get-tuple-element.16, f32[4,128,512]{2,1,0:T(8,128)S(1)} %copy-done.13, f32[4,128,512]{2,1,0:T(8,128)S(1)} %copy-done.12, f32[4,128,512]{2,1,0:T(8,128)S(1)} %copy-done.11, f32[2,1,128,512]{3,2,1,0:T(8,128)} %collective-permute-done.11, ...), kind=kLoop, calls=%fused_computation.66 | loop fusion | flops 5505024 | bytes 10485760 | tf_op jit(solution)/shard_map/sub | solution.py:97
  192.7 0.0 all-reduce.18.cloned.1.call-update
  192.7 75.7 %all-reduce.18.cloned.1.call-done = f32[4,128,512]{2,1,0:T(8,128)} async-done(((f32[4,128,512]{2,1,0:T(8,128)}), f32[4,128,512]{2,1,0:T(8,128)}) %all-reduce.18.cloned.1.call-update) | async-done | bytes 1048592 | tf_op jit(solution)/shard_map/psum | solution.py:106
  268.4 1.6 constant_dynamic-slice_fusion
  270.0 0.0 collective-permute-done.8
  270.0 0.0 collective-permute-done.9
  270.0 19.3 %fusion.13 = f32[1,2,3,4,128,512]{5,4,3,2,1,0:T(8,128)} fusion(f32[2,3,4,128,512]{4,3,2,1,0:T(8,128)} %copy-done.2, f32[2,3,1,128,512]{4,3,2,1,0:T(8,128)} %collective-permute-done.9, f32[2,3,1,128,512]{4,3,2,1,0:T(8,128)} %collective-permute-done.8, f32[1,2,3,4,128,512]{5,4,3,2,1,0:T(8,128)} %param.5, f32[1,3,4,128,512]{4,3,2,1,0:T(8,128)S(1)} %maximum_bitcast_fusion.1, ...), kind=kLoop, calls=%fused_computation.21 | loop fusion | flops 17301504 | bytes 28311552 | tf_op jit(solution)/shard_map/broadcast_in_dim | solution.py:111
  (22 shorter events, 0.1 us)
Async XLA Ops:
  7.2 74.2 %copy-start.16 = (f32[1,4,128,512]{3,2,1,0:T(8,128)S(1)}, f32[1,4,128,512]{3,2,1,0:T(8,128)}, u32[]{:S(2)}) copy-start(f32[1,4,128,512]{3,2,1,0:T(8,128)} %param.4) | copy-start | bytes 3145732
  7.2 34.7 %all-gather.2.cloned.1.call-start = ((), (), s32[]{:S(2)}) async-start(), calls=%async_computation | async-start | bytes 1179648 | tf_op jit(solution)/shard_map/all_gather | solution.py:42
  7.9 260.5 %all-reduce.18.cloned.1.call-start = ((), (), s32[]{:S(2)}) async-start(), calls=%async_computation.1 | async-start | bytes 2097152 | tf_op jit(solution)/shard_map/psum | solution.py:106
  41.9 39.5 %copy-start = (f32[1,2,3,4,128,512]{5,4,3,2,1,0:T(8,128)S(1)}, f32[1,2,3,4,128,512]{5,4,3,2,1,0:T(8,128)}, u32[]{:S(2)}) copy-start(f32[1,2,3,4,128,512]{5,4,3,2,1,0:T(8,128)} %param.5) | copy-start | bytes 18874372
  43.1 11.9 %collective-permute-start.1 = (f32[1,128,512]{2,1,0:T(8,128)S(1)}, f32[1,128,512]{2,1,0:T(8,128)S(1)}, u32[]{:S(2)}, u32[]{:S(2)}) collective-permute-start(f32[1,128,512]{2,1,0:T(8,128)S(1)} %get-tuple-element.35), channel_id=1, source_target_pairs={{1,0},{2,1},{3,2},{4,3},{5,4},{6,5},{7,6},{8,7},{9,8},{10,9},{11,1... | collective-permute-start | bytes 786440 | tf_op jit(solution)/shard_map/ppermute | solution.py:21
  49.0 13.1 %collective-permute-start = (f32[1,128,512]{2,1,0:T(8,128)S(1)}, f32[1,128,512]{2,1,0:T(8,128)S(1)}, u32[]{:S(2)}, u32[]{:S(2)}) collective-permute-start(f32[1,128,512]{2,1,0:T(8,128)S(1)} %get-tuple-element.36), channel_id=1, source_target_pairs={{0,1},{1,2},{2,3},{3,4},{4,5},{5,6},{6,7},{7,8},{8,9},{9,10},{10,1... | collective-permute-start | bytes 786440 | tf_op jit(solution)/shard_map/ppermute | solution.py:20
  62.1 18.1 %copy-start.15 = (f32[1,128,512]{2,1,0:T(8,128)}, f32[1,128,512]{2,1,0:T(8,128)S(1)}, u32[]{:S(2)}) copy-start(f32[1,128,512]{2,1,0:T(8,128)S(1)} %collective-permute-done) | copy-start | bytes 786436
  67.9 12.2 %collective-permute-start.2 = (f32[1,128,512]{2,1,0:T(8,128)S(1)}, f32[1,128,512]{2,1,0:T(8,128)S(1)}, u32[]{:S(2)}, u32[]{:S(2)}) collective-permute-start(f32[1,128,512]{2,1,0:T(8,128)S(1)} %get-tuple-element.33), channel_id=1, source_target_pairs={{0,1},{1,2},{2,3},{3,4},{4,5},{5,6},{6,7},{7,8},{8,9},{9,10},{10,1... | collective-permute-start | bytes 786440 | tf_op jit(solution)/shard_map/ppermute | solution.py:20
  69.9 11.5 %collective-permute-start.3 = (f32[1,128,512]{2,1,0:T(8,128)S(1)}, f32[1,128,512]{2,1,0:T(8,128)S(1)}, u32[]{:S(2)}, u32[]{:S(2)}) collective-permute-start(f32[1,128,512]{2,1,0:T(8,128)S(1)} %get-tuple-element.34), channel_id=1, source_target_pairs={{1,0},{2,1},{3,2},{4,3},{5,4},{6,5},{7,6},{8,7},{9,8},{10,9},{11,1... | collective-permute-start | bytes 786440 | tf_op jit(solution)/shard_map/ppermute | solution.py:21
  84.7 16.6 %collective-permute-start.4 = (f32[2,1,128,512]{3,2,1,0:T(8,128)S(1)}, f32[2,1,128,512]{3,2,1,0:T(8,128)S(1)}, u32[]{:S(2)}, u32[]{:S(2)}) collective-permute-start(f32[2,1,128,512]{3,2,1,0:T(8,128)S(1)} %get-tuple-element.31), channel_id=1, source_target_pairs={{1,0},{2,1},{3,2},{4,3},{5,4},{6,5},{7,6},{8,7},{9,8},{10,9},{11,1... | collective-permute-start | bytes 1572872 | tf_op jit(solution)/shard_map/ppermute | solution.py:21
  92.1 16.3 %collective-permute-start.5 = (f32[2,1,128,512]{3,2,1,0:T(8,128)S(1)}, f32[2,1,128,512]{3,2,1,0:T(8,128)S(1)}, u32[]{:S(2)}, u32[]{:S(2)}) collective-permute-start(f32[2,1,128,512]{3,2,1,0:T(8,128)S(1)} %get-tuple-element.32), channel_id=1, source_target_pairs={{0,1},{1,2},{2,3},{3,4},{4,5},{5,6},{6,7},{7,8},{8,9},{9,10},{10,1... | collective-permute-start | bytes 1572872 | tf_op jit(solution)/shard_map/ppermute | solution.py:20
  101.3 7.1 %copy-start.17 = (f32[2,1,128,512]{3,2,1,0:T(8,128)}, f32[2,1,128,512]{3,2,1,0:T(8,128)S(1)}, u32[]{:S(2)}) copy-start(f32[2,1,128,512]{3,2,1,0:T(8,128)S(1)} %collective-permute-done.4) | copy-start | bytes 1572868
  108.4 0.8 copy-start.18
  109.2 3.6 %copy-start.10 = (f32[4,128,512]{2,1,0:T(8,128)S(1)}, f32[4,128,512]{2,1,0:T(8,128)}, u32[]{:S(2)}) copy-start(f32[4,128,512]{2,1,0:T(8,128)} %all-gather.2.cloned.1.call-done) | copy-start | bytes 3145732
  112.8 3.9 %copy-start.6 = (f32[4,128,512]{2,1,0:T(8,128)}, f32[4,128,512]{2,1,0:T(8,128)S(1)}, u32[]{:S(2)}) copy-start(f32[4,128,512]{2,1,0:T(8,128)S(1)} %get-tuple-element.3) | copy-start | bytes 3145732
  116.8 7.6 %copy-start.8 = (f32[1,4,128,512]{3,2,1,0:T(8,128)}, f32[1,4,128,512]{3,2,1,0:T(8,128)S(1)}, u32[]{:S(2)}) copy-start(f32[1,4,128,512]{3,2,1,0:T(8,128)S(1)} %get-tuple-element.12) | copy-start | bytes 3145732
  117.1 45.7 %copy-start.1 = (f32[1,3,4,128,512]{4,3,2,1,0:T(8,128)}, f32[1,3,4,128,512]{4,3,2,1,0:T(8,128)S(1)}, u32[]{:S(2)}) copy-start(f32[1,3,4,128,512]{4,3,2,1,0:T(8,128)S(1)} %maximum_bitcast_fusion) | copy-start | bytes 9437188
  118.0 39.7 %copy-start.3 = (f32[2,3,4,128,512]{4,3,2,1,0:T(8,128)}, f32[2,3,4,128,512]{4,3,2,1,0:T(8,128)S(1)}, u32[]{:S(2)}) copy-start(f32[2,3,4,128,512]{4,3,2,1,0:T(8,128)S(1)} %fusion.16) | copy-start | bytes 18874372
  118.1 6.3 %copy-start.4 = (f32[1,4,128,512]{3,2,1,0:T(8,128)S(1)}, f32[1,4,128,512]{3,2,1,0:T(8,128)}, u32[]{:S(2)}) copy-start(f32[1,4,128,512]{3,2,1,0:T(8,128)} %get-tuple-element.2) | copy-start | bytes 3145732
  118.4 39.4 %collective-permute-start.6 = (f32[2,3,1,128,512]{4,3,2,1,0:T(8,128)S(1)}, f32[2,3,1,128,512]{4,3,2,1,0:T(8,128)S(1)}, u32[]{:S(2)}, u32[]{:S(2)}) collective-permute-start(f32[2,3,1,128,512]{4,3,2,1,0:T(8,128)S(1)} %get-tuple-element.27), channel_id=1, source_target_pairs={{1,0},{2,1},{3,2},{4,3},{5,4},{6,5},{7,6},{8,7},{9,8},{10,9},{11,1... | collective-permute-start | bytes 4718600 | tf_op jit(solution)/shard_map/ppermute | solution.py:21
  120.4 42.3 %collective-permute-start.7 = (f32[2,3,1,128,512]{4,3,2,1,0:T(8,128)S(1)}, f32[2,3,1,128,512]{4,3,2,1,0:T(8,128)}, u32[]{:S(2)}, u32[]{:S(2)}) collective-permute-start(f32[2,3,1,128,512]{4,3,2,1,0:T(8,128)S(1)} %get-tuple-element.28), channel_id=1, source_target_pairs={{0,1},{1,2},{2,3},{3,4},{4,5},{5,6},{6,7},{7,8},{8,9},{9,10},{10,1... | collective-permute-start | bytes 4718600 | tf_op jit(solution)/shard_map/ppermute | solution.py:20
  125.5 63.0 %collective-permute-start.10 = (f32[2,1,128,512]{3,2,1,0:T(8,128)}, f32[2,1,128,512]{3,2,1,0:T(8,128)}, u32[]{:S(2)}, u32[]{:S(2)}) collective-permute-start(f32[2,1,128,512]{3,2,1,0:T(8,128)} %get-tuple-element.29), channel_id=1, source_target_pairs={{1,0},{2,1},{3,2},{4,3},{5,4},{6,5},{7,6},{8,7},{9,8},{10,9},{11,1... | collective-permute-start | bytes 1572872 | tf_op jit(solution)/shard_map/ppermute | solution.py:21
  130.4 58.1 %collective-permute-start.11 = (f32[2,1,128,512]{3,2,1,0:T(8,128)}, f32[2,1,128,512]{3,2,1,0:T(8,128)}, u32[]{:S(2)}, u32[]{:S(2)}) collective-permute-start(f32[2,1,128,512]{3,2,1,0:T(8,128)} %get-tuple-element.30), channel_id=1, source_target_pairs={{0,1},{1,2},{2,3},{3,4},{4,5},{5,6},{6,7},{7,8},{8,9},{9,10},{10,1... | collective-permute-start | bytes 1572872 | tf_op jit(solution)/shard_map/ppermute | solution.py:20
  157.7 1.2 copy-start.14
  177.4 2.7 copy-start.2
  180.1 8.3 %copy-start.5 = (f32[1,4,128,512]{3,2,1,0:T(8,128)S(1)}, f32[1,4,128,512]{3,2,1,0:T(8,128)}, u32[]{:S(2)}) copy-start(f32[1,4,128,512]{3,2,1,0:T(8,128)} %get-tuple-element.2) | copy-start | bytes 3145732
  180.1 8.3 %copy-start.7 = (f32[4,128,512]{2,1,0:T(8,128)S(1)}, f32[4,128,512]{2,1,0:T(8,128)}, u32[]{:S(2)}) copy-start(f32[4,128,512]{2,1,0:T(8,128)} %copy-done.6) | copy-start | bytes 3145732
  180.1 8.3 %copy-start.9 = (f32[1,4,128,512]{3,2,1,0:T(8,128)S(1)}, f32[1,4,128,512]{3,2,1,0:T(8,128)}, u32[]{:S(2)}) copy-start(f32[1,4,128,512]{3,2,1,0:T(8,128)} %copy-done.8) | copy-start | bytes 3145732
  180.1 8.3 %copy-start.11 = (f32[4,128,512]{2,1,0:T(8,128)S(1)}, f32[4,128,512]{2,1,0:T(8,128)}, u32[]{:S(2)}) copy-start(f32[4,128,512]{2,1,0:T(8,128)} %get-tuple-element.13) | copy-start | bytes 3145732
  180.1 8.4 %copy-start.12 = (f32[4,128,512]{2,1,0:T(8,128)S(1)}, f32[4,128,512]{2,1,0:T(8,128)}, u32[]{:S(2)}) copy-start(f32[4,128,512]{2,1,0:T(8,128)} %get-tuple-element.14) | copy-start | bytes 3145732
  180.1 8.4 %copy-start.13 = (f32[4,128,512]{2,1,0:T(8,128)S(1)}, f32[4,128,512]{2,1,0:T(8,128)}, u32[]{:S(2)}) copy-start(f32[4,128,512]{2,1,0:T(8,128)} %get-tuple-element.15) | copy-start | bytes 3145732
  182.1 87.9 %collective-permute-start.8 = (f32[2,3,1,128,512]{4,3,2,1,0:T(8,128)}, f32[2,3,1,128,512]{4,3,2,1,0:T(8,128)}, u32[]{:S(2)}, u32[]{:S(2)}) collective-permute-start(f32[2,3,1,128,512]{4,3,2,1,0:T(8,128)} %get-tuple-element.25), channel_id=1, source_target_pairs={{1,0},{2,1},{3,2},{4,3},{5,4},{6,5},{7,6},{8,7},{9,8},{10,9},{11,1... | collective-permute-start | bytes 4718600 | tf_op jit(solution)/shard_map/ppermute | solution.py:21
  184.3 85.7 %collective-permute-start.9 = (f32[2,3,1,128,512]{4,3,2,1,0:T(8,128)}, f32[2,3,1,128,512]{4,3,2,1,0:T(8,128)}, u32[]{:S(2)}, u32[]{:S(2)}) collective-permute-start(f32[2,3,1,128,512]{4,3,2,1,0:T(8,128)} %get-tuple-element.26), channel_id=1, source_target_pairs={{0,1},{1,2},{2,3},{3,4},{4,5},{5,6},{6,7},{7,8},{8,9},{9,10},{10,1... | collective-permute-start | bytes 4718600 | tf_op jit(solution)/shard_map/ppermute | solution.py:20
Sparse Core Ops, SparseCore 0:
  9.8 31.9 all-gather.1
  192.8 75.5 all-reduce.17
where the time goes:
time: 297 us; the launch traced here: 296 us
  waiting for transfers between devices  169 us (57%)
  other arithmetic  57.5 us (19%)
  starting transfers between devices  45.2 us (15%)
  between operations  14.4 us (5%)
  local copies, waits for them, and re-layouts  9.79 us (3%)
    psum x1, waiting for transfers between devices, body(): summed = lax.psum(adjoint, 'subj')  75.7 us
    ppermute x6, waiting for transfers between devices, extended_2(): after = lax.ppermute(initial, axis, down)  37.5 us
    all_gather x1, waiting for transfers between devices, body(): whole = lax.all_gather(template, 'subj', axis=1, tiled=True)  33.9 us
    ppermute x6, starting transfers between devices, extended_2(): after = lax.ppermute(initial, axis, down)  29.4 us
    ppermute x6, waiting for transfers between devices, extended_2(): before = lax.ppermute(last, axis, up)  21.5 us
    broadcast_in_dim x1, other arithmetic, body(): return (gradient[None], template_part)  19.3 us
    ppermute x6, starting transfers between devices, extended_2(): before = lax.ppermute(last, axis, up)  15.7 us
    div x1, other arithmetic, body(): smoothed = (source + smooth_weight * beside_all) / scale  14.6 us
  transfers between devices with their start and end apart: 14, of which 10 were waited for; matrix products, arithmetic and copies ran while one was open for 8% of the time, Pallas kernels for 0%

commit v1 on v0

v1 whole, which is shorter than its diff:
```python
import functools

import jax
import jax.numpy as jnp
from jax import lax
from jax.experimental import pallas as pl
from jax.experimental.pallas import tpu as pltpu
from jax.sharding import PartitionSpec as P

MESH = pl.DeviceIdType.MESH
F32 = jnp.float32
DT = 0.5
WEIGHT = -2.5
SEVENTH = 1.0 / 7.0
PAD = 8
R = 16


def kernel(
    nslab, tmpl, subj, vel, out, tg,
    T, I1, L2, L1, S, U, V, V0H, SUB, FS, FR, A0, RB, PS, RZ, TG,
    xs, xr, ts, tr, rs, rr, ls,
):
    ny, nx = tmpl.shape[1] * 8, tmpl.shape[2]
    blk = tmpl.shape[1]
    half = blk // 2
    nchunk = ny // R
    g = lax.axis_index("subj")
    s = lax.axis_index("slab")
    q, c = g // 2, lax.rem(g, 2)
    sib = g + 1 - 2 * c
    has_up, has_dn = s < nslab - 1, s > 0

    def ring(k):
        return 2 * lax.rem(q + k, 4) + c

    def rows(b, n=blk):
        return pl.ds(pl.multiple_of(PAD + b, 8), n)

    body = pl.ds(PAD, ny)
    loads = []
    for t in range(2):
        for d in range(3):
            loads.append(pltpu.make_async_copy(vel.at[0, t, d], V.at[t, d, :, body], ls.at[3 * t + d]))
    loads.append(pltpu.make_async_copy(subj.at[0], SUB, ls.at[6]))
    loads.append(pltpu.make_async_copy(tmpl, T.at[pl.ds(0, 4), rows(g * blk)], ls.at[7]))
    for copy in (loads[7], loads[0], loads[1], loads[2], loads[3], loads[4], loads[5], loads[6]):
        copy.start()

    barrier = pltpu.get_barrier_semaphore()

    def greet(**where):
        pl.semaphore_signal(barrier, inc=1, device_id=where, device_id_type=MESH)

    for peer in (sib, ring(1), ring(2), ring(3)):
        greet(subj=peer)

    greet(slab=lax.rem(s + 1, nslab))
    greet(slab=lax.rem(s + nslab - 1, nslab))

    edge = jnp.zeros((PAD, nx), F32)

    def zero_pads(ref, count):
        def step(p, _):
            ref[p, pl.ds(0, PAD)] = edge
            ref[p, pl.ds(PAD + ny, PAD)] = edge
            return 0

        lax.fori_loop(0, count, step, 0)

    zero_pads(T, 8)
    zero_pads(I1, 6)
    zero_pads(L2, 4)
    zero_pads(L1, 6)
    zero_pads(U, 6)
    for t in range(2):
        zero_pads(V.at[t, 1], 4)
        for d in range(3):
            zero_pads(S.at[t, d], 8)

    def zero_plane(ref, first=0):
        def step(i, _):
            ref[pl.ds(pl.multiple_of(first + i * R, 8), R)] = jnp.zeros((R, nx), F32)
            return 0

        lax.fori_loop(0, nchunk, step, 0)

    def zero_side(side):
        planes, seconds, firsts = ((6, 7), 0, 1) if side == 0 else ((4, 5), 7, 6)
        for p in planes:
            T[p, rows(g * blk)] = jnp.zeros((blk, nx), F32)
        for d in range(3):
            zero_plane(V0H.at[side, d])
            zero_plane(S.at[1, d, seconds], PAD)
            zero_plane(S.at[1, d, firsts], PAD)
            zero_plane(S.at[0, d, seconds], PAD)
        zero_plane(FR.at[side])
        zero_plane(L1.at[0 if side == 0 else 5], PAD)
        zero_plane(U.at[0 if side == 0 else 5], PAD)

    @pl.when(s == 0)
    def _():
        zero_side(0)

    @pl.when(s == nslab - 1)
    def _():
        zero_side(1)

    pl.semaphore_wait(barrier, 6)

    def xcopy(k, dirn):
        up = dirn == 0
        if k == 0:
            src = tmpl.at[pl.ds(2 if up else 0, 2)]
            dst = T.at[pl.ds(6 if up else 4, 2), rows(g * blk)]
        elif k < 4:
            src, dst = vel.at[0, 0, k - 1, 3 if up else 0], V0H.at[dirn, k - 1]
        elif k < 7:
            src, dst = S.at[1, k - 4, 4 if up else 3, body], S.at[1, k - 4, 0 if up else 7, body]
        elif k == 7:
            src, dst = FS.at[dirn], FR.at[dirn]
        elif k < 11:
            src, dst = S.at[1, k - 8, 5 if up else 2, body], S.at[1, k - 8, 1 if up else 6, body]
        elif k == 11:
            src, dst = L1.at[4 if up else 1, body], L1.at[0 if up else 5, body]
        else:
            src, dst = S.at[0, k - 12, 4 if up else 3, body], S.at[0, k - 12, 0 if up else 7, body]
        return pltpu.make_async_remote_copy(
            src, dst, xs.at[dirn, k], xr.at[dirn, k],
            device_id={"slab": s + 1 if up else s - 1}, device_id_type=MESH)

    def xstart(ks):
        @pl.when(has_up)
        def _():
            for k in ks:
                xcopy(k, 0).start()

        @pl.when(has_dn)
        def _():
            for k in ks:
                xcopy(k, 1).start()

    def xrecv(ks):
        @pl.when(has_dn)
        def _():
            for k in ks:
                xcopy(k, 0).wait_recv()

        @pl.when(has_up)
        def _():
            for k in ks:
                xcopy(k, 1).wait_recv()

    def xsent(ks):
        @pl.when(has_up)
        def _():
            for k in ks:
                xcopy(k, 0).wait_send()

        @pl.when(has_dn)
        def _():
            for k in ks:
                xcopy(k, 1).wait_send()

    def tcopy(ph, k, recv=False):
        owner = {0: g, 1: g, 2: ring(3), 3: ring(1), 4: g, 5: ring(3), 6: ring(1), 7: ring(2), 8: ring(2)}[k]
        if recv:
            owner = {0: ring(3), 1: ring(1), 2: ring(2), 3: ring(2)}.get(k, owner + 1 - 2 * c if k > 3 else None)
        off, n = {2: (0, half), 3: (half, half), 7: (0, half), 8: (half, half)}.get(k, (0, blk))
        place = T.at[pl.ds(4 * ph, 4), rows(owner * blk + off, n)]
        src = tmpl if (ph == 0 and k in (0, 1, 4)) else place
        peer = {0: ring(1), 1: ring(3), 2: ring(1), 3: ring(3)}.get(k, sib)
        return pltpu.make_async_remote_copy(
            src, place, ts.at[ph, k], tr.at[ph, k], device_id={"subj": peer}, device_id_type=MESH)

    def twait(ph, k):
        tcopy(ph, k, True).wait_recv()

    xstart((0,))
    for k in (0, 1, 4):
        tcopy(0, k).start()
    xstart((1, 2, 3))
    xrecv((0,))
    for k in (0, 1, 4):
        tcopy(1, k).start()
    for ph in range(2):
        twait(ph, 0)
        tcopy(ph, 2).start()
        tcopy(ph, 5).start()
        twait(ph, 1)
        tcopy(ph, 3).start()
        tcopy(ph, 6).start()
        twait(ph, 2)
        tcopy(ph, 7).start()
        twait(ph, 3)
        tcopy(ph, 8).start()
    for ph in range(2):
        for k in (4, 5, 6, 7, 8):
            twait(ph, k)

    lane = lax.broadcasted_iota(jnp.int32, (R, 128), 1)
    first_lane, last_lane = lane == 0, lane == 127

    def left(x):
        y = pltpu.roll(x, 1, 1)
        return jnp.concatenate([jnp.where(first_lane, 0.0, y[:, :128]), y[:, 128:]], axis=1)

    def right(x):
        y = pltpu.roll(x, nx - 1, 1)
        return jnp.concatenate([y[:, : nx - 128], jnp.where(last_lane, 0.0, y[:, nx - 128 :])], axis=1)

    def chunks(fn):
        def step(i, _):
            fn(pl.multiple_of(i * R, R))
            return 0

        lax.fori_loop(0, nchunk, step, 0)

    def at(ref, r):
        return ref[pl.ds(pl.multiple_of(PAD + r, 8), R)]

    def flat(ref, r):
        return ref[pl.ds(r, R)]

    def around(ref, r):
        ext = ref[pl.ds(r, R + 16)]
        n = R + 16
        return ext[8 : 8 + R], pltpu.roll(ext, 1, 0)[8 : 8 + R], pltpu.roll(ext, n - 1, 0)[8 : 8 + R]

    def put(ref, r, x):
        ref[pl.ds(pl.multiple_of(PAD + r, 8), R)] = x

    def advect(plane, below, above, vread, r):
        here, ym, yp = around(plane, r)
        pairs = ((at(below, r), at(above, r)), (ym, yp), (left(here), right(here)))
        diffs, total = [], None
        for d, (minus, plus) in enumerate(pairs):
            v = vread(d, r)
            diff = jnp.where(v >= 0.0, here - minus, plus - here)
            diffs.append(diff)
            total = v * diff if total is None else total + v * diff
        return here - DT * total, diffs

    def forward_0(z):
        if 0 <= z < 4:
            vread = lambda d, r: at(V.at[0, d, z], r)
        else:
            vread = lambda d, r: flat(V0H.at[0 if z < 0 else 1, d], r)

        def fn(r):
            new, diffs = advect(T.at[z % 8], T.at[(z - 1) % 8], T.at[(z + 1) % 8], vread, r)
            put(I1.at[z + 1], r, new)
            for d in range(3):
                put(S.at[0, d, z + 2], r, WEIGHT * diffs[d])

        chunks(fn)

    def forward_1(z):
        def fn(r):
            vread = lambda d, r: at(V.at[1, d, z], r)
            new, diffs = advect(I1.at[z + 1], I1.at[z], I1.at[z + 2], vread, r)
            lam = new - flat(SUB.at[z], r)
            put(L2.at[z], r, lam)
            scaled = WEIGHT * lam
            for d in range(3):
                put(S.at[1, d, z + 2], r, scaled * diffs[d])
            if z == 0:
                FS[1, pl.ds(r, R)] = jnp.maximum(vread(0, r), 0.0) * lam
            if z == 3:
                FS[0, pl.ds(r, R)] = jnp.minimum(vread(0, r), 0.0) * lam

        chunks(fn)

    def backward(t, lam_ref, z, below, above, r):
        lam = at(lam_ref, r)
        vz = at(V.at[t, 0, z], r)
        total = jnp.abs(vz) * lam - above(r) + below(r)
        vy, lam_ext = V[t, 1, z, pl.ds(r, R + 16)], lam_ref[pl.ds(r, R + 16)]
        pos, neg = jnp.maximum(vy, 0.0) * lam_ext, jnp.minimum(vy, 0.0) * lam_ext
        n = R + 16
        total = total + ((pos - neg)[8 : 8 + R] - pltpu.roll(pos, n - 1, 0)[8 : 8 + R] + pltpu.roll(neg, 1, 0)[8 : 8 + R])
        vx = at(V.at[t, 2, z], r)
        pos, neg = jnp.maximum(vx, 0.0) * lam, jnp.minimum(vx, 0.0) * lam
        total = total + ((pos - neg) - right(pos) + left(neg))
        return lam - DT * total

    def backward_1(z):
        def below(r):
            if z == 0:
                return flat(FR.at[0], r)
            return jnp.minimum(at(V.at[1, 0, z - 1], r), 0.0) * at(L2.at[z - 1], r)

        def above(r):
            if z == 3:
                return flat(FR.at[1], r)
            return jnp.maximum(at(V.at[1, 0, z + 1], r), 0.0) * at(L2.at[z + 1], r)

        def fn(r):
            lam = backward(1, L2.at[z], z, below, above, r)
            put(L1.at[z + 1], r, lam)
            for d in range(3):
                put(S.at[0, d, z + 2], r, at(S.at[0, d, z + 2], r) * lam)

        chunks(fn)

    def backward_0(z):
        def below(r):
            v = flat(V0H.at[0, 0], r) if z == 0 else at(V.at[0, 0, z - 1], r)
            return jnp.minimum(v, 0.0) * at(L1.at[z], r)

        def above(r):
            v = flat(V0H.at[1, 0], r) if z == 3 else at(V.at[0, 0, z + 1], r)
            return jnp.maximum(v, 0.0) * at(L1.at[z + 2], r)

        def fn(r):
            A0[z, pl.ds(r, R)] = backward(0, L1.at[z + 1], z, below, above, r)

        chunks(fn)

    def smooth(t, d):
        def sweep(p, low, high, r):
            here, ym, yp = around(S.at[t, d, p], r)
            beside = ym + yp + left(here) + right(here)
            if low:
                beside = beside + at(S.at[t, d, p - 1], r)
            if high:
                beside = beside + at(S.at[t, d, p + 1], r)
            put(U.at[p - 1], r, (here + beside * SEVENTH) * SEVENTH)

        def inner(p, _):
            chunks(lambda r: sweep(p, True, True, r))
            return 0

        lax.fori_loop(2, 6, inner, 0)

        @pl.when(has_dn)
        def _():
            chunks(lambda r: sweep(1, t == 1, True, r))

        @pl.when(has_up)
        def _():
            chunks(lambda r: sweep(6, True, t == 1, r))

        def last(z, _):
            def fn(r):
                here, ym, yp = around(U.at[z + 1], r)
                beside = ym + yp + left(here) + right(here) + at(U.at[z], r) + at(U.at[z + 2], r)
                put(V.at[t, d, z], r, at(V.at[t, d, z], r) + (at(S.at[t, d, z + 2], r) + beside) * SEVENTH)

            chunks(fn)
            return 0

        lax.fori_loop(0, 4, last, 0)

    def store(t, d):
        return pltpu.make_async_copy(V.at[t, d, :, body], out.at[0, t, d], ls.at[3 * t + d])

    for copy in loads:
        copy.wait()
    for z in range(4):
        forward_0(z)
    forward_1(1)
    forward_1(2)
    xstart((4, 5, 6))
    xrecv((1, 2, 3))
    forward_0(-1)
    forward_0(4)
    forward_1(0)
    forward_1(3)
    xstart((7, 8, 9, 10))
    backward_1(1)
    backward_1(2)
    xrecv((7,))
    backward_1(0)
    backward_1(3)
    xstart((11, 12, 13, 14))
    xrecv((4, 5, 6, 8, 9, 10))

    def smooth_1(d, _):
        smooth(1, d)
        return 0

    lax.fori_loop(0, 3, smooth_1, 0)
    for d in range(3):
        store(1, d).start()
    xrecv((11,))

    for z in range(4):
        backward_0(z)

    def pcopy(k):
        return pltpu.make_async_remote_copy(
            A0.at[:, pl.ds(pl.multiple_of((2 * k + 1 - c) * blk, 8), blk)], RB.at[k], rs.at[k], rr.at[k],
            device_id={"subj": sib}, device_id_type=MESH)

    for k in range(4):
        pcopy(k).start()

    def scale_halo(p, l):
        def fn(r):
            lam = at(L1.at[l], r)
            for d in range(3):
                put(S.at[0, d, p], r, at(S.at[0, d, p], r) * lam)

        chunks(fn)

    scale_halo(1, 0)
    scale_halo(6, 5)
    for k in range(4):
        pcopy(k).wait_recv()

    def pair_sum(k, _):
        for z in range(4):
            PS[k, z] = A0[z, pl.ds(pl.multiple_of((2 * k + c) * blk, 8), blk)] + RB[k, z]
        return 0

    lax.fori_loop(0, 4, pair_sum, 0)

    def zcopy(j):
        return pltpu.make_async_remote_copy(
            PS.at[lax.rem(q + j, 4)], RZ.at[j - 1], rs.at[3 + j], rr.at[3 + j],
            device_id={"subj": ring(j)}, device_id_type=MESH)

    for j in (2, 1, 3):
        zcopy(j).start()

    def smooth_0(d, _):
        smooth(0, d)
        return 0

    lax.fori_loop(0, 3, smooth_0, 0)
    for j in (1, 3, 2):
        zcopy(j).wait_recv()
    for z in range(4):
        TG[z] = PS[q, z] + RZ[0, z] + RZ[1, z] + RZ[2, z]
    tg_copy = pltpu.make_async_copy(TG, tg, ls.at[7])
    tg_copy.start()

    for d in range(3):
        xrecv((12 + d,))

        def fn(r):
            for z, p in ((0, 0), (3, 7)):
                put(V.at[0, d, z], r, at(V.at[0, d, z], r) + at(S.at[0, d, p], r) * (SEVENTH * SEVENTH * SEVENTH))

        chunks(fn)
        store(0, d).start()

    xsent(range(15))
    for ph in range(2):
        for k in range(9):
            tcopy(ph, k).wait_send()
    for k in range(4):
        pcopy(k).wait_send()
    for j in range(1, 4):
        zcopy(j).wait_send()
    tg_copy.wait()
    for t in range(2):
        for d in range(3):
            store(t, d).wait()


def body(nslab, template, subject, velocity):
    depth, blk, nx = template.shape
    ny = subject.shape[2]
    tall = ny + 2 * PAD
    vmem = lambda *shape: pltpu.VMEM(shape, F32)
    dma = lambda *shape: pltpu.SemaphoreType.DMA(shape)
    return pl.pallas_call(
        functools.partial(kernel, nslab),
        out_shape=(
            jax.ShapeDtypeStruct(velocity.shape, F32),
            jax.ShapeDtypeStruct(template.shape, F32),
        ),
        in_specs=[pl.BlockSpec(memory_space=pl.ANY)] * 3,
        out_specs=(pl.BlockSpec(memory_space=pl.ANY),) * 2,
        scratch_shapes=[
            vmem(8, tall, nx),
            vmem(6, tall, nx),
            vmem(4, tall, nx),
            vmem(6, tall, nx),
            vmem(2, 3, 8, tall, nx),
            vmem(6, tall, nx),
            vmem(2, 3, 4, tall, nx),
            vmem(2, 3, ny, nx),
            vmem(4, ny, nx),
            vmem(2, ny, nx),
            vmem(2, ny, nx),
            vmem(4, ny, nx),
            vmem(4, 4, blk, nx),
            vmem(4, 4, blk, nx),
            vmem(3, 4, blk, nx),
            vmem(4, blk, nx),
            dma(2, 15), dma(2, 15), dma(2, 9), dma(2, 9), dma(7), dma(7), dma(8),
        ],
        compiler_params=pltpu.CompilerParams(
            collective_id=0, has_side_effects=True, vmem_limit_bytes=56 << 20),
    )(template, subject, velocity)


def solution(mesh):
    return jax.shard_map(
        functools.partial(body, mesh.shape["slab"]),
        mesh=mesh,
        in_specs=(
            P("slab", "subj", None),
            P("subj", "slab", None, None),
            P("subj", None, None, "slab", None, None),
        ),
        out_specs=(P("subj", None, None, "slab", None, None), P("slab", "subj", None)),
        check_vma=False,
    )
```

time: 297 us -> 156 us (0.53)
  waiting for transfers between devices: 169 us -> 0 us
  Pallas kernels: 0 us -> 148 us
  other arithmetic: 57.5 us -> 0 us
  starting transfers between devices: 45.2 us -> 0 us
  between operations: 14.4 us -> 0.65 us
    pallas_call x0 -> x1, Pallas kernels: none -> 148 us  [body(): pl.pallas_call(functools.partial(kernel, nslab), out_shape=(jax.ShapeDtyp...]
    psum x1 -> x0, waiting for transfers between devices: 75.7 us -> none  [body(): summed = lax.psum(adjoint, 'subj')]
    ppermute x12 -> x0, waiting for transfers between devices: 59 us -> none  [the longest x6 37.5 us: extended_2(): after = lax.ppermute(initial, axis, down)]
    ppermute x12 -> x0, starting transfers between devices: 45.1 us -> none  [the longest x6 29.4 us: extended_2(): after = lax.ppermute(initial, axis, down)]
    all_gather x1 -> x0, waiting for transfers between devices: 33.9 us -> none  [body(): whole = lax.all_gather(template, 'subj', axis=1, tiled=True)]
    broadcast_in_dim x1 -> x0, other arithmetic: 19.3 us -> none  [body(): return (gradient[None], template_part)]
    div x2 -> x0, other arithmetic: 15.6 us -> none  [the longest x1 14.6 us: body(): smoothed = (source + smooth_weight * beside_all) / scale]
    another operation x6 -> x0, other arithmetic: 11.5 us -> none  [the longest x3 9.14 us: body(): jnp.stack([positives[0], negatives[0]])]
  transfers between devices with their start and end apart: 14 -> 0, of which waited for: 10 -> 0; matrix products, arithmetic and copies ran while one was open for 8% -> 0% of each run, Pallas kernels for 0% -> 0%
where the time goes in v1:
time: 156 us; the launch traced here: 155 us
  Pallas kernels  148 us (95%)
  local copies, waits for them, and re-layouts  7.26 us (5%)
    pallas_call x1, Pallas kernels, body(): pl.pallas_call(functools.partial(kernel, nslab), out_shape=(jax.ShapeDtyp...  148 us
    unnamed x4, local copies, waits for them, and re-layouts  7.26 us

profile of v1, /device:TPU:24, one launch (start us, length us, event | category | flops | bytes accessed | tf_op | source)
XLA Modules:
  0.0 155.4 jit_solution(4781890434007927278)
XLA Ops:
  0.6 147.5 %shard_map.50 = (f32[1,2,3,4,128,512]{5,4,3,2,1,0:T(8,128)}, f32[4,16,512]{2,1,0:T(8,128)}) custom-call(f32[4,16,512]{2,1,0:T(8,128)} %tmpl.1, f32[1,4,128,512]{3,2,1,0:T(8,128)} %subj.1, f32[1,2,3,4,128,512]{5,4,3,2,1,0:T(8,128)} %vel.1), custom_call_target="tpu_custom_call" | custom-call | tf_op jit(solution)/shard_map/pallas_call | solution.py:469
  148.2 0.0 copy-start
  148.2 6.6 %copy.7 = f32[1,2,3,4,128,512]{5,4,3,2,1,0:T(8,128)} copy(f32[1,2,3,4,128,512]{5,4,3,2,1,0:T(8,128)} %get-tuple-element.4) | data formatting | bytes 12582912
  154.8 0.0 copy-done
  154.8 0.7 copy.8
Async XLA Ops:
  148.2 6.6 %copy-start = (f32[4,16,512]{2,1,0:T(8,128)S(1)}, f32[4,16,512]{2,1,0:T(8,128)}, u32[]{:S(2)}) copy-start(f32[4,16,512]{2,1,0:T(8,128)} %get-tuple-element.5) | copy-start | bytes 393220

commit v2 on v1

--- a/solution.py
+++ b/solution.py
@@ -13,7 +13,7 @@
 WEIGHT = -2.5
 SEVENTH = 1.0 / 7.0
 PAD = 8
-R = 16
+R = 64
 
 
 def kernel(
@@ -88,7 +88,8 @@
     def zero_side(side):
         planes, seconds, firsts = ((6, 7), 0, 1) if side == 0 else ((4, 5), 7, 6)
         for p in planes:
-            T[p, rows(g * blk)] = jnp.zeros((blk, nx), F32)
+            for k in range(4):
+                T[p, rows((2 * k + c) * blk)] = jnp.zeros((blk, nx), F32)
         for d in range(3):
             zero_plane(V0H.at[side, d])
             zero_plane(S.at[1, d, seconds], PAD)
@@ -110,9 +111,10 @@
 
     def xcopy(k, dirn):
         up = dirn == 0
-        if k == 0:
-            src = tmpl.at[pl.ds(2 if up else 0, 2)]
-            dst = T.at[pl.ds(6 if up else 4, 2), rows(g * blk)]
+        if k == 0 or k > 14:
+            place = rows((g if k == 0 else ring((3, 1, 2)[k - 15])) * blk)
+            src = tmpl.at[pl.ds(2 if up else 0, 2)] if k == 0 else T.at[pl.ds(2 if up else 0, 2), place]
+            dst = T.at[pl.ds(6 if up else 4, 2), place]
         elif k < 4:
             src, dst = vel.at[0, 0, k - 1, 3 if up else 0], V0H.at[dirn, k - 1]
         elif k < 7:
@@ -162,41 +164,52 @@
             for k in ks:
                 xcopy(k, 1).wait_send()
 
-    def tcopy(ph, k, recv=False):
+    def tcopy(k, recv=False):
         owner = {0: g, 1: g, 2: ring(3), 3: ring(1), 4: g, 5: ring(3), 6: ring(1), 7: ring(2), 8: ring(2)}[k]
         if recv:
-            owner = {0: ring(3), 1: ring(1), 2: ring(2), 3: ring(2)}.get(k, owner + 1 - 2 * c if k > 3 else None)
+            owner = {0: ring(3), 1: ring(1), 2: ring(2), 3: ring(2)}.get(k, owner + 1 - 2 * c)
         off, n = {2: (0, half), 3: (half, half), 7: (0, half), 8: (half, half)}.get(k, (0, blk))
-        place = T.at[pl.ds(4 * ph, 4), rows(owner * blk + off, n)]
-        src = tmpl if (ph == 0 and k in (0, 1, 4)) else place
+        place = T.at[pl.ds(0, 4), rows(owner * blk + off, n)]
+        src = tmpl if k in (0, 1, 4) else place
         peer = {0: ring(1), 1: ring(3), 2: ring(1), 3: ring(3)}.get(k, sib)
         return pltpu.make_async_remote_copy(
-            src, place, ts.at[ph, k], tr.at[ph, k], device_id={"subj": peer}, device_id_type=MESH)
-
-    def twait(ph, k):
-        tcopy(ph, k, True).wait_recv()
+            src, place, ts.at[0, k], tr.at[0, k], device_id={"subj": peer}, device_id_type=MESH)
+
+    def hcopy(j, recv=False):
+        owner = (g, ring(3), ring(1), ring(2))[j]
+        if recv:
+            owner = owner + 1 - 2 * c
+        place = T.at[pl.ds(4, 4), rows(owner * blk)]
+        return pltpu.make_async_remote_copy(
+            place, place, ts.at[1, j], tr.at[1, j], device_id={"subj": sib}, device_id_type=MESH)
+
+    def twait(k):
+        tcopy(k, True).wait_recv()
 
     xstart((0,))
     for k in (0, 1, 4):
-        tcopy(0, k).start()
-    xstart((1, 2, 3))
-    xrecv((0,))
-    for k in (0, 1, 4):
-        tcopy(1, k).start()
-    for ph in range(2):
-        twait(ph, 0)
-        tcopy(ph, 2).start()
-        tcopy(ph, 5).start()
-        twait(ph, 1)
-        tcopy(ph, 3).start()
-        tcopy(ph, 6).start()
-        twait(ph, 2)
-        tcopy(ph, 7).start()
-        twait(ph, 3)
-        tcopy(ph, 8).start()
-    for ph in range(2):
-        for k in (4, 5, 6, 7, 8):
-            twait(ph, k)
+        tcopy(k).start()
+    xstart((1,))
+    twait(0)
+    tcopy(2).start()
+    xstart((15,))
+    tcopy(5).start()
+    twait(1)
+    tcopy(3).start()
+    xstart((16, 2))
+    tcopy(6).start()
+    twait(2)
+    tcopy(7).start()
+    twait(3)
+    xstart((17, 3))
+    tcopy(8).start()
+    for j, k in enumerate((0, 15, 16, 17)):
+        xrecv((k,))
+        hcopy(j).start()
+    for k in (4, 5, 6, 7, 8):
+        twait(k)
+    for j in range(4):
+        hcopy(j, True).wait_recv()
 
     lane = lax.broadcasted_iota(jnp.int32, (R, 128), 1)
     first_lane, last_lane = lane == 0, lane == 127
@@ -345,15 +358,12 @@
             def fn(r):
                 here, ym, yp = around(U.at[z + 1], r)
                 beside = ym + yp + left(here) + right(here) + at(U.at[z], r) + at(U.at[z + 2], r)
-                put(V.at[t, d, z], r, at(V.at[t, d, z], r) + (at(S.at[t, d, z + 2], r) + beside) * SEVENTH)
+                out[0, t, d, z, pl.ds(r, R)] = at(V.at[t, d, z], r) + (at(S.at[t, d, z + 2], r) + beside) * SEVENTH
 
             chunks(fn)
             return 0
 
         lax.fori_loop(0, 4, last, 0)
-
-    def store(t, d):
-        return pltpu.make_async_copy(V.at[t, d, :, body], out.at[0, t, d], ls.at[3 * t + d])
 
     for copy in loads:
         copy.wait()
@@ -381,8 +391,6 @@
         return 0
 
     lax.fori_loop(0, 3, smooth_1, 0)
-    for d in range(3):
-        store(1, d).start()
     xrecv((11,))
 
     for z in range(4):
@@ -441,23 +449,21 @@
 
         def fn(r):
             for z, p in ((0, 0), (3, 7)):
-                put(V.at[0, d, z], r, at(V.at[0, d, z], r) + at(S.at[0, d, p], r) * (SEVENTH * SEVENTH * SEVENTH))
+                late = at(S.at[0, d, p], r) * (SEVENTH * SEVENTH * SEVENTH)
+                out[0, 0, d, z, pl.ds(r, R)] = out[0, 0, d, z, pl.ds(r, R)] + late
 
         chunks(fn)
-        store(0, d).start()
-
-    xsent(range(15))
-    for ph in range(2):
-        for k in range(9):
-            tcopy(ph, k).wait_send()
+
+    xsent(range(18))
+    for k in range(9):
+        tcopy(k).wait_send()
+    for j in range(4):
+        hcopy(j).wait_send()
     for k in range(4):
         pcopy(k).wait_send()
     for j in range(1, 4):
         zcopy(j).wait_send()
     tg_copy.wait()
-    for t in range(2):
-        for d in range(3):
-            store(t, d).wait()
 
 
 def body(nslab, template, subject, velocity):
@@ -472,8 +478,8 @@
             jax.ShapeDtypeStruct(velocity.shape, F32),
             jax.ShapeDtypeStruct(template.shape, F32),
         ),
-        in_specs=[pl.BlockSpec(memory_space=pl.ANY)] * 3,
-        out_specs=(pl.BlockSpec(memory_space=pl.ANY),) * 2,
+        in_specs=[pl.BlockSpec(memory_space=pltpu.HBM)] * 3,
+        out_specs=(pl.BlockSpec(memory_space=pltpu.VMEM), pl.BlockSpec(memory_space=pl.ANY)),
         scratch_shapes=[
             vmem(8, tall, nx),
             vmem(6, tall, nx),
@@ -491,11 +497,11 @@
             vmem(4, 4, blk, nx),
             vmem(3, 4, blk, nx),
             vmem(4, blk, nx),
-            dma(2, 15), dma(2, 15), dma(2, 9), dma(2, 9), dma(7), dma(7), dma(8),
+            dma(2, 18), dma(2, 18), dma(2, 9), dma(2, 9), dma(7), dma(7), dma(8),
         ],
         compiler_params=pltpu.CompilerParams(
-            collective_id=0, has_side_effects=True, vmem_limit_bytes=56 << 20),
-    )(template, subject, velocity)
+            collective_id=0, has_side_effects=True, vmem_limit_bytes=40 << 20),
+    )(*(pltpu.with_memory_space_constraint(x, pltpu.HBM) for x in (template, subject, velocity)))
 
 
 def solution(mesh):

time: 156 us -> 121 us (0.78)
  Pallas kernels: 148 us -> 116 us
  local copies, waits for them, and re-layouts: 7.26 us -> 3.36 us
    pallas_call x1, Pallas kernels: 148 us -> 116 us  [body(): pl.pallas_call(functools.partial(kernel, nslab), out_shape=(jax.ShapeDtyp...]
    unnamed x4 -> x2, local copies, waits for them, and re-layouts: 7.26 us -> 3.36 us
where the time goes in v2:
time: 121 us; the launch traced here: 120 us
  Pallas kernels  116 us (96%)
  local copies, waits for them, and re-layouts  3.36 us (3%)
    pallas_call x1, Pallas kernels, body(): pl.pallas_call(functools.partial(kernel, nslab), out_shape=(jax.ShapeDtyp...  116 us
    unnamed x2, local copies, waits for them, and re-layouts  3.36 us

profile of v2, /device:TPU:24, one launch (start us, length us, event | category | flops | bytes accessed | tf_op | source)
XLA Modules:
  0.0 120.5 jit_solution(2796785186984542239)
XLA Ops:
  0.6 116.5 %shard_map.50 = (f32[1,2,3,4,128,512]{5,4,3,2,1,0:T(8,128)S(1)}, f32[4,16,512]{2,1,0:T(8,128)S(1)}) custom-call(f32[4,16,512]{2,1,0:T(8,128)} %tmpl.1, f32[1,4,128,512]{3,2,1,0:T(8,128)} %subj.1, f32[1,2,3,4,128,512]{5,4,3,2,1,0:T(8,128)} %vel.1), custom_call_target="tpu_custom_call" | custom-call | tf_op jit(solution)/shard_map/pallas_call | solution.py:475
  117.1 2.7 %copy.7 = f32[1,2,3,4,128,512]{5,4,3,2,1,0:T(8,128)} copy(f32[1,2,3,4,128,512]{5,4,3,2,1,0:T(8,128)S(1)} %get-tuple-element.4) | data formatting | bytes 12582912
  119.8 0.7 copy.8

commit v3 on v2

--- a/solution.py
+++ b/solution.py
@@ -18,8 +18,8 @@
 
 def kernel(
     nslab, tmpl, subj, vel, out, tg,
-    T, I1, L2, L1, S, U, V, V0H, SUB, FS, FR, A0, RB, PS, RZ, TG,
-    xs, xr, ts, tr, rs, rr, ls,
+    T, I1, L2, L1, S, U, V, V0H, SUB, FS, FR, A0, RB, PS, RH, RZ, TG, GPS, GRH, GRZ, TG2,
+    xs, xr, ts, tr, rs, rr, gs, gr, ls,
 ):
     ny, nx = tmpl.shape[1] * 8, tmpl.shape[2]
     blk = tmpl.shape[1]
@@ -111,7 +111,7 @@
 
     def xcopy(k, dirn):
         up = dirn == 0
-        if k == 0 or k > 14:
+        if k == 0 or 14 < k < 18:
             place = rows((g if k == 0 else ring((3, 1, 2)[k - 15])) * blk)
             src = tmpl.at[pl.ds(2 if up else 0, 2)] if k == 0 else T.at[pl.ds(2 if up else 0, 2), place]
             dst = T.at[pl.ds(6 if up else 4, 2), place]
@@ -131,16 +131,19 @@
             src, dst, xs.at[dirn, k], xr.at[dirn, k],
             device_id={"slab": s + 1 if up else s - 1}, device_id_type=MESH)
 
-    def xstart(ks):
-        @pl.when(has_up)
+    def xeach(ks, up, dn, fn):
+        @pl.when(up)
         def _():
             for k in ks:
-                xcopy(k, 0).start()
-
-        @pl.when(has_dn)
+                fn(xcopy(k, 0))
+
+        @pl.when(dn)
         def _():
             for k in ks:
-                xcopy(k, 1).start()
+                fn(xcopy(k, 1))
+
+    def xstart(ks, up=has_up, dn=has_dn):
+        xeach(ks, up, dn, lambda copy: copy.start())
 
     def xrecv(ks):
         @pl.when(has_dn)
@@ -153,16 +156,8 @@
             for k in ks:
                 xcopy(k, 1).wait_recv()
 
-    def xsent(ks):
-        @pl.when(has_up)
-        def _():
-            for k in ks:
-                xcopy(k, 0).wait_send()
-
-        @pl.when(has_dn)
-        def _():
-            for k in ks:
-                xcopy(k, 1).wait_send()
+    def xsent(ks, up=has_up, dn=has_dn):
+        xeach(ks, up, dn, lambda copy: copy.wait_send())
 
     def tcopy(k, recv=False):
         owner = {0: g, 1: g, 2: ring(3), 3: ring(1), 4: g, 5: ring(3), 6: ring(1), 7: ring(2), 8: ring(2)}[k]
@@ -186,22 +181,28 @@
     def twait(k):
         tcopy(k, True).wait_recv()
 
+    cross_up, cross_dn = has_up & (lax.rem(s, 4) == 3), has_dn & (lax.rem(s, 4) == 0)
+    near_up, near_dn = has_up & (lax.rem(s, 4) != 3), has_dn & (lax.rem(s, 4) != 0)
+
     xstart((0,))
     for k in (0, 1, 4):
         tcopy(k).start()
-    xstart((1,))
+    xstart((1,), near_up, near_dn)
     twait(0)
     tcopy(2).start()
     xstart((15,))
     tcopy(5).start()
     twait(1)
     tcopy(3).start()
-    xstart((16, 2))
+    xstart((16,))
+    xstart((2,), near_up, near_dn)
     tcopy(6).start()
     twait(2)
     tcopy(7).start()
     twait(3)
-    xstart((17, 3))
+    xstart((17,))
+    xstart((3,), near_up, near_dn)
+    xstart((1, 2, 3), cross_up, cross_dn)
     tcopy(8).start()
     for j, k in enumerate((0, 15, 16, 17)):
         xrecv((k,))
@@ -371,26 +372,25 @@
         forward_0(z)
     forward_1(1)
     forward_1(2)
-    xstart((4, 5, 6))
+    xstart((4, 5))
     xrecv((1, 2, 3))
     forward_0(-1)
     forward_0(4)
     forward_1(0)
     forward_1(3)
-    xstart((7, 8, 9, 10))
+    xstart((7,))
     backward_1(1)
     backward_1(2)
+    xsent((4,))
+    xstart((6,))
     xrecv((7,))
     backward_1(0)
     backward_1(3)
-    xstart((11, 12, 13, 14))
-    xrecv((4, 5, 6, 8, 9, 10))
-
-    def smooth_1(d, _):
-        smooth(1, d)
-        return 0
-
-    lax.fori_loop(0, 3, smooth_1, 0)
+    xstart((11,))
+    xsent((5,))
+    xstart((8,))
+    xsent((6,))
+    xstart((9,))
     xrecv((11,))
 
     for z in range(4):
@@ -424,23 +424,103 @@
 
     lax.fori_loop(0, 4, pair_sum, 0)
 
-    def zcopy(j):
-        return pltpu.make_async_remote_copy(
-            PS.at[lax.rem(q + j, 4)], RZ.at[j - 1], rs.at[3 + j], rr.at[3 + j],
-            device_id={"subj": ring(j)}, device_id_type=MESH)
-
-    for j in (2, 1, 3):
-        zcopy(j).start()
-
-    def smooth_0(d, _):
-        smooth(0, d)
+    turn = lax.rem(s, 4)
+    is_host = (turn == 1) | (turn == 2)
+    is_guest = (turn == 0) | (turn == 3)
+    partner = s + 1 - 2 * lax.rem(turn, 2)
+
+    def gcopy(j):
+        return pltpu.make_async_remote_copy(
+            PS.at[lax.rem(q + j, 4)], GPS.at[lax.rem(q + j, 4)], gs.at[j], gr.at[j],
+            device_id={"slab": partner}, device_id_type=MESH)
+
+    def give_back():
+        return pltpu.make_async_remote_copy(
+            TG2, RZ.at[0], gs.at[0], gr.at[0], device_id={"slab": partner}, device_id_type=MESH)
+
+    def hsum(j, o):
+        return pltpu.make_async_remote_copy(
+            (PS, GPS)[o].at[lax.rem(q + 2, 4), :, pl.ds(half * j, half)], (RH, GRH)[o].at[j],
+            rs.at[4 + 4 * o + j], rr.at[4 + 4 * o + j], device_id={"subj": ring((1, 3)[j])}, device_id_type=MESH)
+
+    def zcopy(j, o):
+        return pltpu.make_async_remote_copy(
+            (PS, GPS)[o].at[lax.rem(q + (1, 3)[j], 4)], (RZ, GRZ)[o].at[j],
+            rs.at[6 + 4 * o + j], rr.at[6 + 4 * o + j], device_id={"subj": ring((1, 3)[j])}, device_id_type=MESH)
+
+    def ring_start(o):
+        for j in range(2):
+            hsum(j, o).start()
+
+    def ring_next(o):
+        ref, got = (PS, GPS)[o], (RH, GRH)[o]
+        for j in range(2):
+            hsum(j, o).wait_recv()
+            k = lax.rem(q + (1, 3)[j], 4)
+            for z in range(4):
+                ref[k, z, pl.ds(half * j, half)] = ref[k, z, pl.ds(half * j, half)] + got[j, z]
+            zcopy(j, o).start()
+
+    held_up, held_dn = has_up & (turn == 0), has_dn & (turn == 3)
+    free_up, free_dn = has_up & (turn != 0), has_dn & (turn != 3)
+
+    @pl.when(is_guest)
+    def _():
+        for j in (2, 1, 3):
+            gcopy(j).start()
+
+    @pl.when(is_host)
+    def _():
+        ring_start(0)
+
+    xstart((10, 12, 13, 14), free_up, free_dn)
+    smooth(0, 0)
+
+    @pl.when(is_host)
+    def _():
+        ring_next(0)
+        gcopy(2).wait_recv()
+        ring_start(1)
+
+    xsent((8,), held_up, held_dn)
+    xstart((10,), held_up, held_dn)
+    smooth(0, 1)
+
+    @pl.when(is_host)
+    def _():
+        gcopy(1).wait_recv()
+        gcopy(3).wait_recv()
+        ring_next(1)
+
+    xstart((12,), held_up, held_dn)
+    smooth(0, 2)
+    xstart((13, 14), held_up, held_dn)
+
+    @pl.when(is_host)
+    def _():
+        for o in range(2):
+            for j in range(2):
+                zcopy(j, o).wait_recv()
+        for z in range(4):
+            TG2[z] = GRZ[0, z] + GRZ[1, z]
+        give_back().start()
+        for z in range(4):
+            TG[z] = PS[q, z] + RZ[0, z] + RZ[1, z]
+
+    xrecv((4, 5, 6, 8, 9, 10))
+
+    def smooth_1(d, _):
+        smooth(1, d)
         return 0
 
-    lax.fori_loop(0, 3, smooth_0, 0)
-    for j in (1, 3, 2):
-        zcopy(j).wait_recv()
-    for z in range(4):
-        TG[z] = PS[q, z] + RZ[0, z] + RZ[1, z] + RZ[2, z]
+    lax.fori_loop(0, 3, smooth_1, 0)
+
+    @pl.when(is_guest)
+    def _():
+        give_back().wait_recv()
+        for z in range(4):
+            TG[z] = PS[q, z] + RZ[0, z]
+
     tg_copy = pltpu.make_async_copy(TG, tg, ls.at[7])
     tg_copy.start()
 
@@ -454,15 +534,28 @@
 
         chunks(fn)
 
-    xsent(range(18))
+    xsent((0, 1, 2, 3, 7, 9, 10, 11, 12, 13, 14, 15, 16, 17))
+    xsent((8,), free_up, free_dn)
     for k in range(9):
         tcopy(k).wait_send()
     for j in range(4):
         hcopy(j).wait_send()
     for k in range(4):
         pcopy(k).wait_send()
-    for j in range(1, 4):
-        zcopy(j).wait_send()
+
+    @pl.when(is_host)
+    def _():
+        for o in range(2):
+            for j in range(2):
+                hsum(j, o).wait_send()
+                zcopy(j, o).wait_send()
+        give_back().wait_send()
+
+    @pl.when(is_guest)
+    def _():
+        for j in range(1, 4):
+            gcopy(j).wait_send()
+
     tg_copy.wait()
 
 
@@ -495,9 +588,14 @@
             vmem(4, ny, nx),
             vmem(4, 4, blk, nx),
             vmem(4, 4, blk, nx),
-            vmem(3, 4, blk, nx),
+            vmem(2, 4, blk // 2, nx),
+            vmem(2, 4, blk, nx),
             vmem(4, blk, nx),
-            dma(2, 18), dma(2, 18), dma(2, 9), dma(2, 9), dma(7), dma(7), dma(8),
+            vmem(4, 4, blk, nx),
+            vmem(2, 4, blk // 2, nx),
+            vmem(2, 4, blk, nx),
+            vmem(4, blk, nx),
+            dma(2, 18), dma(2, 18), dma(2, 9), dma(2, 9), dma(12), dma(12), dma(4), dma(4), dma(8),
         ],
         compiler_params=pltpu.CompilerParams(
             collective_id=0, has_side_effects=True, vmem_limit_bytes=40 << 20),

time: 121 us -> 115 us (0.950)
  Pallas kernels: 116 us -> 109 us
    pallas_call x1, Pallas kernels: 116 us -> 109 us  [body(): pl.pallas_call(functools.partial(kernel, nslab), out_shape=(jax.ShapeDtyp...]
where the time goes in v3:
time: 115 us; the launch traced here: 113 us
  Pallas kernels  109 us (95%)
  local copies, waits for them, and re-layouts  3.36 us (3%)
    pallas_call x1, Pallas kernels, body(): pl.pallas_call(functools.partial(kernel, nslab), out_shape=(jax.ShapeDtyp...  109 us
    unnamed x2, local copies, waits for them, and re-layouts  3.36 us

profile of v3, /device:TPU:24, one launch (start us, length us, event | category | flops | bytes accessed | tf_op | source)
XLA Modules:
  0.0 113.4 jit_solution(3920879614708974302)
XLA Ops:
  0.6 109.4 %shard_map.50 = (f32[1,2,3,4,128,512]{5,4,3,2,1,0:T(8,128)S(1)}, f32[4,16,512]{2,1,0:T(8,128)S(1)}) custom-call(f32[4,16,512]{2,1,0:T(8,128)} %tmpl.1, f32[1,4,128,512]{3,2,1,0:T(8,128)} %subj.1, f32[1,2,3,4,128,512]{5,4,3,2,1,0:T(8,128)} %vel.1), custom_call_target="tpu_custom_call" | custom-call | tf_op jit(solution)/shard_map/pallas_call | solution.py:568
  110.1 2.7 %copy.7 = f32[1,2,3,4,128,512]{5,4,3,2,1,0:T(8,128)} copy(f32[1,2,3,4,128,512]{5,4,3,2,1,0:T(8,128)S(1)} %get-tuple-element.4) | data formatting | bytes 12582912
  112.8 0.7 copy.8

commit v4 on v3

--- a/solution.py
+++ b/solution.py
@@ -559,13 +559,24 @@
     tg_copy.wait()
 
 
+def write_out(grad_ref, part_ref, grad_out, part_out, sems):
+    n = 6
+    copies = [pltpu.make_async_copy(part_ref, part_out, sems.at[n])]
+    for i in range(n):
+        copies.append(pltpu.make_async_copy(grad_ref.at[0, i // 3, i % 3], grad_out.at[0, i // 3, i % 3], sems.at[i]))
+    for copy in copies:
+        copy.start()
+    for copy in copies:
+        copy.wait()
+
+
 def body(nslab, template, subject, velocity):
     depth, blk, nx = template.shape
     ny = subject.shape[2]
     tall = ny + 2 * PAD
     vmem = lambda *shape: pltpu.VMEM(shape, F32)
     dma = lambda *shape: pltpu.SemaphoreType.DMA(shape)
-    return pl.pallas_call(
+    results = pl.pallas_call(
         functools.partial(kernel, nslab),
         out_shape=(
             jax.ShapeDtypeStruct(velocity.shape, F32),
@@ -600,6 +611,17 @@
         compiler_params=pltpu.CompilerParams(
             collective_id=0, has_side_effects=True, vmem_limit_bytes=40 << 20),
     )(*(pltpu.with_memory_space_constraint(x, pltpu.HBM) for x in (template, subject, velocity)))
+    return pl.pallas_call(
+        write_out,
+        out_shape=(
+            jax.ShapeDtypeStruct(velocity.shape, F32),
+            jax.ShapeDtypeStruct(template.shape, F32),
+        ),
+        in_specs=[pl.BlockSpec(memory_space=pltpu.VMEM)] * 2,
+        out_specs=(pl.BlockSpec(memory_space=pltpu.HBM),) * 2,
+        scratch_shapes=[dma(7)],
+        compiler_params=pltpu.CompilerParams(vmem_limit_bytes=16 << 20),
+    )(*results)
 
 
 def solution(mesh):

time: 115 us -> 114 us (level)
  local copies, waits for them, and re-layouts: 3.36 us -> 0 us
  Pallas kernels: 109 us -> 112 us
    unnamed x2 -> x0, local copies, waits for them, and re-layouts: 3.36 us -> none
    pallas_call x0 -> x1, Pallas kernels: none -> 2.77 us  [body(): pl.pallas_call(write_out, out_shape=(jax.ShapeDtypeStruct(velocity.shape,...]
where the time goes in v4:
time: 114 us; the launch traced here: 113 us
  Pallas kernels  112 us (98%)
    pallas_call x1, Pallas kernels, body(): pl.pallas_call(functools.partial(kernel, nslab), out_shape=(jax.ShapeDtyp...  109 us
    pallas_call x1, Pallas kernels, body(): pl.pallas_call(write_out, out_shape=(jax.ShapeDtypeStruct(velocity.shape,...  2.77 us

profile of v4, /device:TPU:24, one launch (start us, length us, event | category | flops | bytes accessed | tf_op | source)
XLA Modules:
  0.0 112.9 jit_solution(15380373335097591545)
XLA Ops:
  0.6 109.4 %shard_map.50 = (f32[1,2,3,4,128,512]{5,4,3,2,1,0:T(8,128)S(1)}, f32[4,16,512]{2,1,0:T(8,128)S(1)}) custom-call(f32[4,16,512]{2,1,0:T(8,128)} %tmpl.1, f32[1,4,128,512]{3,2,1,0:T(8,128)} %subj.1, f32[1,2,3,4,128,512]{5,4,3,2,1,0:T(8,128)} %vel.1), custom_call_target="tpu_custom_call" | custom-call | tf_op jit(solution)/shard_map/pallas_call | solution.py:579
  110.1 2.8 %shard_map.51 = (f32[1,2,3,4,128,512]{5,4,3,2,1,0:T(8,128)}, f32[4,16,512]{2,1,0:T(8,128)}) custom-call(f32[1,2,3,4,128,512]{5,4,3,2,1,0:T(8,128)S(1)} %get-tuple-element.4.grad_ref, f32[4,16,512]{2,1,0:T(8,128)S(1)} %get-tuple-element.5.part_ref), custom_call_target="tpu_custom_call" | custom-call | tf_op jit(solution)/shard_map/pallas_call | solution.py:614
